TPU v7x, 512 devices: a whole 4x8x8 slice. The times are simulated.
512 devices in a mesh: fsdp: 64 (over y_lo, z, core), tp: 8 (over x, y_hi).
Axes of the slice: x: 4, y: 8 (y_hi: 2, y_lo: 4; y = y_hi * 4 + y_lo), z: 8, core: 2. Of those that a mesh axis runs over, the one named last changes fastest.
Arguments:
- images: bfloat16 [64, 256, 6144], P('fsdp', None, 'tp'), may hold values from -6 to 6
- keep_index: int32 [64, 64], P('fsdp'), may hold values from 0 to 255, as said below
- teacher_weight: float32 [6144, 3072], P('fsdp', 'tp'), may hold values from -0.078125 to 0.078125
- student_weight: float32 [6144, 3072], P('fsdp', 'tp'), may hold values from -0.078125 to 0.078125
Outputs:
- teacher_next: float32 [6144, 3072], P('fsdp', 'tp')
- student_grad: float32 [6144, 3072], P('fsdp', 'tp')
Inputs may be any that keep to these rules, and one draw needn't show every extreme that they name: `keep_index`: each image's 64 indices are distinct and increasing.
All inputs are finite; a program needn't handle non-finite values.
Results may differ from a plain program's by a relative error of at most 0.0048.
Values may be sent and summed in bfloat16 or wider, within the bound.
No kernel may reach another device: no remote copies, remote signals or barrier semaphores. Data moves between devices by JAX's collectives and lax.ppermute only.
A program may use at most 64 MiB of HBM per device.

v0:
```python
import math
import jax
import jax.numpy as jnp
from jax import lax
from jax.sharding import PartitionSpec as P

D = 6144


def layer_norm(values):
    floats = values.astype(jnp.float32)
    centre = jnp.mean(floats, axis=-1, keepdims=True)
    centred = floats - centre
    spread = jnp.mean(centred * centred, axis=-1, keepdims=True)
    return (centred * lax.rsqrt(spread + 1e-06)).astype(jnp.bfloat16)


def pick_rows(table, index):
    return jax.vmap(lambda block, rows: block[rows])(table, index)


def row_product(features, piece):
    return jnp.dot(features, piece, preferred_element_type=jnp.float32)


def shards(images, keep_index, teacher_weight, student_weight):
    img_count = images.shape[0]
    patch_count = images.shape[1]
    keep_count = keep_index.shape[1]
    columns_dev = teacher_weight.shape[1]
    teacher_next = 0.999 * teacher_weight + (1.0 - 0.999) * student_weight
    teacher_panel = teacher_next.astype(jnp.bfloat16)
    student_panel = student_weight.astype(jnp.bfloat16)
    whole = lax.all_gather(images, "tp", axis=2, tiled=True)
    normed = layer_norm(whole)
    flat_all = normed.reshape(img_count * patch_count, D)
    picked = pick_rows(normed, keep_index).reshape(img_count * keep_count, D)
    teacher_out = row_product(flat_all, lax.all_gather(teacher_panel, "fsdp", axis=0, tiled=True))
    student_out = row_product(picked, lax.all_gather(student_panel, "fsdp", axis=0, tiled=True))
    teacher_out = teacher_out.reshape(img_count, patch_count, columns_dev)
    centre = jnp.mean(teacher_out, axis=1, keepdims=True)
    centred_out = teacher_out - centre
    spread = jnp.mean(centred_out * centred_out, axis=1, keepdims=True)
    target = centred_out * lax.rsqrt(spread + 1e-05)
    target_kept = pick_rows(target, keep_index).reshape(img_count * keep_count, columns_dev)
    total_kept = img_count * keep_count * lax.axis_size("fsdp")
    error = ((student_out - target_kept) * (1.0 / math.sqrt(total_kept))).astype(jnp.bfloat16)
    owned = lax.all_to_all(picked, "fsdp", split_axis=1, concat_axis=0, tiled=True)
    student_grad = lax.dot_general(
        owned,
        lax.all_gather(error, "fsdp", axis=0, tiled=True),
        (((0,), (0,)), ((), ())),
        preferred_element_type=jnp.float32,
    )
    return (teacher_next, student_grad)


def solution(mesh):
    placed = (P("fsdp", None, "tp"), P("fsdp", None), P("fsdp", "tp"), P("fsdp", "tp"))
    return jax.shard_map(
        shards,
        mesh=mesh,
        in_specs=placed,
        out_specs=(P("fsdp", "tp"), P("fsdp", "tp")),
        check_vma=False,
    )
```

profile of v0, /device:TPU:1, one launch (start us, length us, event | category | flops | bytes accessed | tf_op | source)
XLA Modules:
  0.0 498.9 jit_solution(11816537188644948361)
XLA Ops:
  7.2 0.0 all-gather.5.cloned.1.call-start
  7.2 0.7 all-gather.5.cloned.1.call-update
  7.9 0.0 all-gather.9.cloned.1.call-start
  7.9 1.8 fusion.9
  9.7 0.0 all-gather.9.cloned.1.call-update
  9.7 0.0 all-gather.7.cloned.1.call-start
  9.8 0.7 all-gather.7.cloned.1.call-update
  10.5 0.0 all-gather.11.cloned.1.call-start
  10.5 0.7 fusion.8
  11.2 97.9 %all-gather.5.cloned.1.call-done = bf16[1,256,6144]{2,1,0:T(8,128)(2,1)} async-done(((bf16[1,256,768]{2,1,0:T(8,128)(2,1)}), bf16[1,256,6144]{2,1,0:T(8,128)(2,1)}) %all-gather.5.cloned.1.call-update) | async-done | bytes 3145744 | tf_op jit(solution)/shard_map/all_gather | solution.py:34
  109.1 0.0 copy-start
  109.1 2.5 convert_reduce_fusion
  111.7 0.3 copy-done
  111.9 1.0 fusion.2
  112.9 1.2 fusion.3
  114.1 3.8 gather_fusion
  117.9 114.0 %all-gather.9.cloned.1.call-done = bf16[6144,384]{1,0:T(8,128)(2,1)} async-done(((bf16[96,384]{1,0:T(8,128)(2,1)}), bf16[6144,384]{1,0:T(8,128)(2,1)}) %all-gather.9.cloned.1.call-update) | async-done | bytes 4718608 | tf_op jit(solution)/shard_map/all_gather | solution.py:38
  231.9 4.3 fusion.10
  236.2 0.0 copy-start.1
  236.2 0.1 multiply_reduce_fusion
  236.3 0.8 gather_fusion.1
  237.1 116.3 %all-gather.7.cloned.1.call-done = bf16[6144,384]{1,0:T(8,128)(2,1)} async-done(((bf16[96,384]{1,0:T(8,128)(2,1)}), bf16[6144,384]{1,0:T(8,128)(2,1)}) %all-gather.7.cloned.1.call-update) | async-done | bytes 4718608 | tf_op jit(solution)/shard_map/all_gather | solution.py:39
  353.4 4.0 fusion.7
  357.4 0.0 all-gather.11.cloned.1.call-update
  357.4 0.0 copy-done.1
  357.4 1.0 all_to_all.14
  358.5 0.7 copy.6
  359.2 36.8 %all_to_all.19 = bf16[64,64,96]{2,0,1:T(8,128)(2,1)S(1)} all-to-all(bf16[64,64,96]{2,0,1:T(8,128)(2,1)S(1)} %copy.6), channel_id=1, replica_groups=mesh['fsdp'=64,'tp'=8] {'fsdp'}, dimensions={1} | all-to-all | bytes 1572864 | tf_op jit(solution)/shard_map/all_to_all | solution.py:48
  396.0 93.2 %all-gather.11.cloned.1.call-done = bf16[4096,384]{1,0:T(8,128)(2,1)} async-done(((bf16[64,384]{1,0:T(8,128)(2,1)}), bf16[4096,384]{1,0:T(8,128)(2,1)}) %all-gather.11.cloned.1.call-update) | async-done | bytes 3145744 | tf_op jit(solution)/shard_map/all_gather | solution.py:51
  489.2 3.3 fusion.11
  (7 shorter events, 0.1 us)
Async XLA Ops:
  7.2 101.9 %all-gather.5.cloned.1.call-start = ((), (), s32[]{:S(2)}) async-start(), calls=%async_computation.1 | async-start | bytes 3538944 | tf_op jit(solution)/shard_map/all_gather | solution.py:34
  7.9 224.0 %all-gather.9.cloned.1.call-start = ((), (), s32[]{:S(2)}) async-start(), calls=%async_computation.3 | async-start | bytes 4792320 | tf_op jit(solution)/shard_map/all_gather | solution.py:38
  9.7 343.6 %all-gather.7.cloned.1.call-start = ((), (), s32[]{:S(2)}) async-start(), calls=%async_computation.2 | async-start | bytes 4792320 | tf_op jit(solution)/shard_map/all_gather | solution.py:39
  10.5 478.7 %all-gather.11.cloned.1.call-start = ((), (), s32[]{:S(2)}) async-start(), calls=%async_computation.4 | async-start | bytes 3194880 | tf_op jit(solution)/shard_map/all_gather | solution.py:51
  109.1 2.8 copy-start
  236.2 121.3 %copy-start.1 = (bf16[64,6144]{1,0:T(8,128)(2,1)S(1)}, bf16[64,6144]{1,0:T(8,128)(2,1)}, u32[]{:S(2)}) copy-start(bf16[64,6144]{1,0:T(8,128)(2,1)} %gather_fusion) | copy-start | bytes 2359300
Sparse Core Ops, SparseCore 0:
  11.1 97.9 all-gather.4
  111.8 120.0 all-gather.8
  234.0 119.2 all-gather.6
  357.5 131.5 all-gather.10
where the time goes:
time: 499 us
  waiting for transfers between devices  423 us (85%)
  blocking collectives  36.8 us (7%)
  between operations  13.8 us (3%)
  matrix products  11.5 us (2%)
  other arithmetic  7.33 us (1%)
  local copies, waits for them, and re-layouts  6.58 us (1%)
    all_gather x1, waiting for transfers between devices, shards(): lax.all_gather(student_panel, 'fsdp', axis=0, tiled=True)  116 us
    all_gather x1, waiting for transfers between devices, shards(): lax.all_gather(teacher_panel, 'fsdp', axis=0, tiled=True)  114 us
    all_gather x1, waiting for transfers between devices, shards(): whole = lax.all_gather(images, 'tp', axis=2, tiled=True)  97.9 us
    all_gather x1, waiting for transfers between devices, shards(): lax.all_gather(error, 'fsdp', axis=0, tiled=True)  93.2 us
    all_to_all x1, blocking collectives, shards(): lax.all_to_all(picked, 'fsdp', split_axis=1, concat_axis=0, tiled=True)  36.8 us
  transfers between devices with their start and end apart: 4, of which 4 were waited for; matrix products, arithmetic and copies ran while one was open for 3% of the time, Pallas kernels for 0%

commit v1 on v0

--- a/solution.py
+++ b/solution.py
@@ -5,6 +5,13 @@
 from jax.sharding import PartitionSpec as P
 
 D = 6144
+
+
+def exchange_blocks(x, mesh_axis, split, join):
+    size = lax.axis_size(mesh_axis)
+    pieces = jnp.stack(jnp.split(x, size, axis=split), axis=0)
+    pieces = lax.all_to_all(pieces, mesh_axis, split_axis=0, concat_axis=0)
+    return jnp.concatenate(pieces, axis=join)
 
 
 def layer_norm(values):
@@ -45,7 +52,7 @@
     target_kept = pick_rows(target, keep_index).reshape(img_count * keep_count, columns_dev)
     total_kept = img_count * keep_count * lax.axis_size("fsdp")
     error = ((student_out - target_kept) * (1.0 / math.sqrt(total_kept))).astype(jnp.bfloat16)
-    owned = lax.all_to_all(picked, "fsdp", split_axis=1, concat_axis=0, tiled=True)
+    owned = exchange_blocks(picked, "fsdp", 1, 0)
     student_grad = lax.dot_general(
         owned,
         lax.all_gather(error, "fsdp", axis=0, tiled=True),

time: 499 us -> 507 us (1.016); the launches traced: 499 us -> 500 us
  local copies, waits for them, and re-layouts: 6.58 us -> 94 us
  waiting for transfers between devices: 423 us -> 336 us
    unnamed x4 -> x65, local copies, waits for them, and re-layouts: 0.29 us -> 88.1 us
    all_gather x1, waiting for transfers between devices: 114 us -> 53.9 us  [shards(): lax.all_gather(teacher_panel, 'fsdp', axis=0, tiled=True)]
    all_gather x1, waiting for transfers between devices: 93.2 us -> 66.3 us  [shards(): lax.all_gather(error, 'fsdp', axis=0, tiled=True)]
  transfers between devices with their start and end apart: 4 -> 4, of which waited for: 4 -> 4; matrix products, arithmetic and copies ran while one was open for 3% -> 21% of each run, Pallas kernels for 0% -> 0%
where the time goes in v1:
time: 507 us; the launch traced here: 500 us
  waiting for transfers between devices  336 us (66%)
  local copies, waits for them, and re-layouts  94 us (19%)
  blocking collectives  37.4 us (7%)
  between operations  13.8 us (3%)
  matrix products  11.5 us (2%)
  other arithmetic  7.34 us (1%)
    all_gather x1, waiting for transfers between devices, shards(): lax.all_gather(student_panel, 'fsdp', axis=0, tiled=True)  117 us
    all_gather x1, waiting for transfers between devices, shards(): whole = lax.all_gather(images, 'tp', axis=2, tiled=True)  97.9 us
    unnamed x65, local copies, waits for them, and re-layouts  88.1 us
    all_gather x1, waiting for transfers between devices, shards(): lax.all_gather(error, 'fsdp', axis=0, tiled=True)  66.3 us
    all_gather x1, waiting for transfers between devices, shards(): lax.all_gather(teacher_panel, 'fsdp', axis=0, tiled=True)  53.9 us
    all_to_all x1, blocking collectives, exchange_blocks(): pieces = lax.all_to_all(pieces, mesh_axis, split_axis=0, concat_axis=0)  37.4 us
  transfers between devices with their start and end apart: 4, of which 4 were waited for; matrix products, arithmetic and copies ran while one was open for 21% of the time, Pallas kernels for 0%

profile of v1, /device:TPU:1, one launch (start us, length us, event | category | flops | bytes accessed | tf_op | source)
XLA Modules:
  0.0 500.4 jit_solution(13496221525428990058)
XLA Ops:
  7.9 1.8 fusion.9
  11.2 97.9 %all-gather.5.cloned.1.call-done = bf16[1,256,6144]{2,1,0:T(8,128)(2,1)} async-done(((bf16[1,256,768]{2,1,0:T(8,128)(2,1)}), bf16[1,256,6144]{2,1,0:T(8,128)(2,1)}) %all-gather.5.cloned.1.call-update) | async-done | bytes 3145744 | tf_op jit(solution)/shard_map/all_gather | solution.py:41
  109.1 2.5 convert_reduce_fusion
  114.1 3.8 gather_fusion
  119.2 1.4 constant_dynamic-update-slice_fusion.62
  120.7 1.4 constant_dynamic-update-slice_fusion.61
  122.1 1.4 constant_dynamic-update-slice_fusion.60
  124.8 1.4 constant_dynamic-update-slice_fusion.58
  126.3 1.4 constant_dynamic-update-slice_fusion.57
  127.7 1.4 constant_dynamic-update-slice_fusion.56
  130.4 1.4 constant_dynamic-update-slice_fusion.54
  131.8 1.4 constant_dynamic-update-slice_fusion.53
  133.3 1.4 constant_dynamic-update-slice_fusion.52
  134.6 1.3 constant_dynamic-update-slice_fusion.51
  136.0 1.4 constant_dynamic-update-slice_fusion.50
  137.4 1.4 constant_dynamic-update-slice_fusion.49
  138.8 1.4 constant_dynamic-update-slice_fusion.48
  141.6 1.4 constant_dynamic-update-slice_fusion.46
  143.0 1.4 constant_dynamic-update-slice_fusion.45
  144.4 1.4 constant_dynamic-update-slice_fusion.44
  147.1 1.4 constant_dynamic-update-slice_fusion.42
  148.6 1.4 constant_dynamic-update-slice_fusion.41
  150.0 1.4 constant_dynamic-update-slice_fusion.40
  151.4 1.3 constant_dynamic-update-slice_fusion.39
  152.7 1.4 constant_dynamic-update-slice_fusion.38
  154.1 1.4 constant_dynamic-update-slice_fusion.37
  155.6 1.4 constant_dynamic-update-slice_fusion.36
  157.0 1.3 constant_dynamic-update-slice_fusion.35
  158.3 1.4 constant_dynamic-update-slice_fusion.34
  159.7 1.4 constant_dynamic-update-slice_fusion.33
  161.2 1.4 constant_dynamic-update-slice_fusion.32
  163.9 1.4 constant_dynamic-update-slice_fusion.30
  165.3 1.4 constant_dynamic-update-slice_fusion.29
  166.7 1.4 constant_dynamic-update-slice_fusion.28
  168.1 1.3 constant_dynamic-update-slice_fusion.27
  169.4 1.4 constant_dynamic-update-slice_fusion.26
  170.9 1.4 constant_dynamic-update-slice_fusion.25
  172.3 1.4 constant_dynamic-update-slice_fusion.24
  175.0 1.4 constant_dynamic-update-slice_fusion.22
  176.4 1.4 constant_dynamic-update-slice_fusion.21
  177.9 53.9 %all-gather.9.cloned.1.call-done = bf16[6144,384]{1,0:T(8,128)(2,1)} async-done(((bf16[96,384]{1,0:T(8,128)(2,1)}), bf16[6144,384]{1,0:T(8,128)(2,1)}) %all-gather.9.cloned.1.call-update) | async-done | bytes 4718608 | tf_op jit(solution)/shard_map/all_gather | solution.py:45
  231.8 4.3 fusion.10
  237.0 116.6 %all-gather.7.cloned.1.call-done = bf16[6144,384]{1,0:T(8,128)(2,1)} async-done(((bf16[96,384]{1,0:T(8,128)(2,1)}), bf16[6144,384]{1,0:T(8,128)(2,1)}) %all-gather.7.cloned.1.call-update) | async-done | bytes 4718608 | tf_op jit(solution)/shard_map/all_gather | solution.py:46
  353.6 4.0 fusion.7
  357.6 1.4 constant_dynamic-update-slice_fusion.20
  360.3 1.4 constant_dynamic-update-slice_fusion.18
  361.7 1.4 constant_dynamic-update-slice_fusion.17
  363.2 1.4 constant_dynamic-update-slice_fusion.16
  365.9 1.4 constant_dynamic-update-slice_fusion.14
  367.3 1.4 constant_dynamic-update-slice_fusion.13
  368.8 1.4 constant_dynamic-update-slice_fusion.12
  371.5 1.4 constant_dynamic-update-slice_fusion.10
  372.9 1.4 constant_dynamic-update-slice_fusion.9
  374.3 1.4 constant_dynamic-update-slice_fusion.8
  375.7 1.3 constant_dynamic-update-slice_fusion.7
  377.0 1.4 constant_dynamic-update-slice_fusion.6
  378.5 1.4 constant_dynamic-update-slice_fusion.5
  379.9 1.4 constant_dynamic-update-slice_fusion.4
  382.6 1.4 constant_dynamic-update-slice_fusion.2
  384.0 1.4 constant_dynamic-update-slice_fusion.1
  385.5 1.4 constant_dynamic-update-slice_fusion
  386.9 37.4 %all_to_all.5 = bf16[64,64,96]{2,1,0:T(8,128)(2,1)S(1)} all-to-all(bf16[64,64,96]{2,1,0:T(8,128)(2,1)} %constant_dynamic-update-slice_fusion), channel_id=1, replica_groups=mesh['fsdp'=64,'tp'=8] {'fsdp'}, dimensions={0} | all-to-all | bytes 1572864 | tf_op jit(solution)/shard_map/all_to_all | solution.py:13
  424.3 66.3 %all-gather.11.cloned.1.call-done = bf16[4096,384]{1,0:T(8,128)(2,1)} async-done(((bf16[64,384]{1,0:T(8,128)(2,1)}), bf16[4096,384]{1,0:T(8,128)(2,1)}) %all-gather.11.cloned.1.call-update) | async-done | bytes 3145744 | tf_op jit(solution)/shard_map/all_gather | solution.py:58
  490.6 3.3 fusion.11
  (33 shorter events, 20.1 us)
Async XLA Ops:
  7.2 101.9 %all-gather.5.cloned.1.call-start = ((), (), s32[]{:S(2)}) async-start(), calls=%async_computation.1 | async-start | bytes 3538944 | tf_op jit(solution)/shard_map/all_gather | solution.py:41
  7.9 223.9 %all-gather.9.cloned.1.call-start = ((), (), s32[]{:S(2)}) async-start(), calls=%async_computation.3 | async-start | bytes 4792320 | tf_op jit(solution)/shard_map/all_gather | solution.py:45
  9.8 343.8 %all-gather.7.cloned.1.call-start = ((), (), s32[]{:S(2)}) async-start(), calls=%async_computation.2 | async-start | bytes 4792320 | tf_op jit(solution)/shard_map/all_gather | solution.py:46
  10.5 480.1 %all-gather.11.cloned.1.call-start = ((), (), s32[]{:S(2)}) async-start(), calls=%async_computation.4 | async-start | bytes 3194880 | tf_op jit(solution)/shard_map/all_gather | solution.py:58
  109.1 2.8 copy-start
Sparse Core Ops, SparseCore 0:
  11.1 97.9 all-gather.4
  111.8 119.9 all-gather.8
  233.9 119.5 all-gather.6
  357.7 132.8 all-gather.10

commit v2 on v0

--- a/solution.py
+++ b/solution.py
@@ -5,6 +5,13 @@
 from jax.sharding import PartitionSpec as P
 
 D = 6144
+
+
+def swapped_in(x, name, dim):
+    devices = lax.axis_size(name)
+    tiles = jnp.stack([x for _ in range(devices)])
+    tiles = lax.all_to_all(tiles, name, split_axis=0, concat_axis=0)
+    return jnp.concatenate(tiles, axis=dim)
 
 
 def layer_norm(values):
@@ -35,7 +42,7 @@
     normed = layer_norm(whole)
     flat_all = normed.reshape(img_count * patch_count, D)
     picked = pick_rows(normed, keep_index).reshape(img_count * keep_count, D)
-    teacher_out = row_product(flat_all, lax.all_gather(teacher_panel, "fsdp", axis=0, tiled=True))
+    teacher_out = row_product(flat_all, swapped_in(teacher_panel, "fsdp", 0))
     student_out = row_product(picked, lax.all_gather(student_panel, "fsdp", axis=0, tiled=True))
     teacher_out = teacher_out.reshape(img_count, patch_count, columns_dev)
     centre = jnp.mean(teacher_out, axis=1, keepdims=True)

time: 499 us -> 431 us (0.86); the launches traced: 499 us -> 426 us
  waiting for transfers between devices: 423 us -> 330 us
  starting transfers between devices: 0.16 us -> 15.8 us
    all_gather x1 -> x0, waiting for transfers between devices: 114 us -> none  [shards(): lax.all_gather(teacher_panel, 'fsdp', axis=0, tiled=True)]
    all_to_all x0 -> x1, waiting for transfers between devices: none -> 32.7 us  [swapped_in(): tiles = lax.all_to_all(tiles, name, split_axis=0, concat_axis=0)]
    all_gather x1, waiting for transfers between devices: 116 us -> 94.7 us  [shards(): lax.all_gather(student_panel, 'fsdp', axis=0, tiled=True)]
    all_to_all x0 -> x1, starting transfers between devices: none -> 15.7 us  [swapped_in(): tiles = lax.all_to_all(tiles, name, split_axis=0, concat_axis=0)]
    all_gather x1, waiting for transfers between devices: 97.9 us -> 109 us  [shards(): whole = lax.all_gather(images, 'tp', axis=2, tiled=True)]
  transfers between devices with their start and end apart: 4 -> 4, of which waited for: 4 -> 4; matrix products, arithmetic and copies ran while one was open for 3% -> 4% of each run, Pallas kernels for 0% -> 0%
where the time goes in v2:
time: 431 us; the launch traced here: 426 us
  waiting for transfers between devices  330 us (77%)
  blocking collectives  38.1 us (9%)
  starting transfers between devices  15.8 us (4%)
  between operations  13.8 us (3%)
  matrix products  11.6 us (3%)
  local copies, waits for them, and re-layouts  9.27 us (2%)
  other arithmetic  6.66 us (2%)
    all_gather x1, waiting for transfers between devices, shards(): whole = lax.all_gather(images, 'tp', axis=2, tiled=True)  109 us
    all_gather x1, waiting for transfers between devices, shards(): lax.all_gather(student_panel, 'fsdp', axis=0, tiled=True)  94.7 us
    all_gather x1, waiting for transfers between devices, shards(): lax.all_gather(error, 'fsdp', axis=0, tiled=True)  92.9 us
    all_to_all x1, blocking collectives, shards(): lax.all_to_all(picked, 'fsdp', split_axis=1, concat_axis=0, tiled=True)  38.1 us
    all_to_all x1, waiting for transfers between devices, swapped_in(): tiles = lax.all_to_all(tiles, name, split_axis=0, concat_axis=0)  32.7 us
    all_to_all x1, starting transfers between devices, swapped_in(): tiles = lax.all_to_all(tiles, name, split_axis=0, concat_axis=0)  15.7 us
  transfers between devices with their start and end apart: 4, of which 4 were waited for; matrix products, arithmetic and copies ran while one was open for 4% of the time, Pallas kernels for 0%

profile of v2, /device:TPU:1, one launch (start us, length us, event | category | flops | bytes accessed | tf_op | source)
XLA Modules:
  0.0 425.8 jit_solution(15391939949036122785)
XLA Ops:
  7.2 0.0 all-gather.4.cloned.1.call-start
  7.2 0.7 all-gather.4.cloned.1.call-update
  7.9 1.8 fusion.9
  9.7 2.7 stack.2
  12.3 0.0 copy-start.2
  12.3 15.7 %all-to-all-start.1 = ((bf16[64,96,384]{2,1,0:T(8,128)(2,1)}), bf16[64,96,384]{2,1,0:T(8,128)(2,1)}, u32[]{:S(2)}, u32[]{:S(2)}) async-start(bf16[64,96,384]{2,1,0:T(8,128)(2,1)} %stack.2), calls=%async_computation.1 | async-start | bytes 9437184 | tf_op jit(solution)/shard_map/all_to_all | solution.py:13
  28.0 0.0 all-gather.6.cloned.1.call-start
  28.1 0.7 all-gather.6.cloned.1.call-update
  28.8 0.0 all-gather.8.cloned.1.call-start
  28.8 0.0 copy-done.2
  28.9 108.8 %all-gather.4.cloned.1.call-done = bf16[1,256,6144]{2,1,0:T(8,128)(2,1)} async-done(((bf16[1,256,768]{2,1,0:T(8,128)(2,1)}), bf16[1,256,6144]{2,1,0:T(8,128)(2,1)}) %all-gather.4.cloned.1.call-update) | async-done | bytes 3145744 | tf_op jit(solution)/shard_map/all_gather | solution.py:41
  137.7 0.0 copy-start
  137.7 2.5 convert_reduce_fusion
  140.3 0.3 copy-done
  140.6 1.0 fusion.2
  141.5 1.2 fusion.3
  142.8 3.8 gather_fusion
  146.6 32.7 %all-to-all-done.1 = bf16[64,96,384]{2,1,0:T(8,128)(2,1)} async-done(((bf16[64,96,384]{2,1,0:T(8,128)(2,1)}), bf16[64,96,384]{2,1,0:T(8,128)(2,1)}, u32[]{:S(2)}, u32[]{:S(2)}) %all-to-all-start.1) | async-done | bytes 4718624 | tf_op jit(solution)/shard_map/all_to_all | solution.py:13
  179.3 4.3 %fusion.10 = (f32[384]{0:T(512)S(1)}, f32[256,384]{1,0:T(8,128)S(1)}) fusion(bf16[6144,384]{1,0:T(8,128)(2,1)} %bitcast.6, bf16[1,256,6144]{2,1,0:T(8,128)(2,1)S(1)} %fusion.3), kind=kOutput, calls=%fused_computation.25 | convolution fusion | flops 1208057472 | bytes 8259072 | tf_op jit(solution)/shard_map/dot_general | solution.py:30
  183.6 0.0 copy-start.1
  183.6 0.1 multiply_reduce_fusion
  183.7 0.8 gather_fusion.1
  184.5 94.7 %all-gather.6.cloned.1.call-done = bf16[6144,384]{1,0:T(8,128)(2,1)} async-done(((bf16[96,384]{1,0:T(8,128)(2,1)}), bf16[6144,384]{1,0:T(8,128)(2,1)}) %all-gather.6.cloned.1.call-update) | async-done | bytes 4718608 | tf_op jit(solution)/shard_map/all_gather | solution.py:46
  279.2 4.0 fusion.7
  283.2 0.0 all-gather.8.cloned.1.call-update
  283.2 0.0 copy-done.1
  283.2 1.0 all_to_all.17
  284.3 0.7 copy.6
  285.0 38.1 %all_to_all.24 = bf16[64,64,96]{2,0,1:T(8,128)(2,1)S(1)} all-to-all(bf16[64,64,96]{2,0,1:T(8,128)(2,1)S(1)} %copy.6), channel_id=1, replica_groups=mesh['fsdp'=64,'tp'=8] {'fsdp'}, dimensions={1} | all-to-all | bytes 1572864 | tf_op jit(solution)/shard_map/all_to_all | solution.py:55
  323.1 92.9 %all-gather.8.cloned.1.call-done = bf16[4096,384]{1,0:T(8,128)(2,1)} async-done(((bf16[64,384]{1,0:T(8,128)(2,1)}), bf16[4096,384]{1,0:T(8,128)(2,1)}) %all-gather.8.cloned.1.call-update) | async-done | bytes 3145744 | tf_op jit(solution)/shard_map/all_gather | solution.py:58
  416.0 3.2 fusion.11
  (8 shorter events, 0.1 us)
Async XLA Ops:
  7.2 130.6 %all-gather.4.cloned.1.call-start = ((), (), s32[]{:S(2)}) async-start(), calls=%async_computation.2 | async-start | bytes 3538944 | tf_op jit(solution)/shard_map/all_gather | solution.py:41
  12.3 16.5 %copy-start.2 = (s32[1,64]{1,0:T(1,128)S(1)}, s32[1,64]{1,0:T(1,128)}, u32[]{:S(2)}) copy-start(s32[1,64]{1,0:T(1,128)} %param.5) | copy-start | bytes 772
  12.3 166.9 %all-to-all-start.1 = ((bf16[64,96,384]{2,1,0:T(8,128)(2,1)}), bf16[64,96,384]{2,1,0:T(8,128)(2,1)}, u32[]{:S(2)}, u32[]{:S(2)}) async-start(bf16[64,96,384]{2,1,0:T(8,128)(2,1)} %stack.2), calls=%async_computation.1 | async-start | bytes 9437184 | tf_op jit(solution)/shard_map/all_to_all | solution.py:13
  28.0 251.2 %all-gather.6.cloned.1.call-start = ((), (), s32[]{:S(2)}) async-start(), calls=%async_computation.3 | async-start | bytes 4792320 | tf_op jit(solution)/shard_map/all_gather | solution.py:46
  28.8 387.2 %all-gather.8.cloned.1.call-start = ((), (), s32[]{:S(2)}) async-start(), calls=%async_computation.4 | async-start | bytes 3194880 | tf_op jit(solution)/shard_map/all_gather | solution.py:58
  137.7 2.8 copy-start
  183.6 99.7 %copy-start.1 = (bf16[64,6144]{1,0:T(8,128)(2,1)S(1)}, bf16[64,6144]{1,0:T(8,128)(2,1)}, u32[]{:S(2)}) copy-start(bf16[64,6144]{1,0:T(8,128)(2,1)} %gather_fusion) | copy-start | bytes 2359300
Sparse Core Ops, SparseCore 0:
  11.1 126.5 all-gather.3
  140.4 138.7 all-gather.5
  283.4 132.5 all-gather.7
